TPU v7x, 32 devices: a whole 2x2x4 slice. The times are simulated.
32 devices in a mesh: dp: 4 (over x, core), ctx: 2 (over y), head: 4 (over z).
Axes of the slice: x: 2, y: 2, z: 4, core: 2. Of those that a mesh axis runs over, the one named last changes fastest.
Arguments:
- inputs: bfloat16 [16, 256, 1024], P('dp', 'ctx', 'head'), parts along dimension 0, may hold values from -6 to 6
- lengths: int32 [16], P('dp'), parts along dimension 0, may hold values from 1 to 640, 1024 in all
- proj_in: bfloat16 [1024, 4, 1024], P(None, None, 'head'), may hold values from -0.1875 to 0.1875
- proj_out: bfloat16 [1024, 1024], P('head'), may hold values from -0.1875 to 0.1875
Outputs:
- layer_out: bfloat16 [8, 2, 256, 1024], P(('dp', 'ctx'), None, None, 'head'), parts along dimension 0
There are 4 independent parts, one for each index of `dp`. A program takes and returns all parts, laid end to end along the dimension named above; an argument that names none is the same for every part. Nothing has to cross between parts.
Inputs may be any that keep to these rules, and one draw needn't show every extreme that they name: The 4 histories lie end to end in the packed rows; the lengths sum to 1024 and the longest is exactly 640.
All inputs are finite; a program needn't handle non-finite values.
Results may differ from a plain program's by a relative error of at most 0.0055.
Values may be sent and summed in bfloat16 or wider, within the bound.
No kernel may reach another device: no remote copies, remote signals or barrier semaphores. Data moves between devices by JAX's collectives and lax.ppermute only.
A program may use at most 64 MiB of HBM per device.

v0:
```python
import math
import jax
import jax.numpy as jnp
from jax import lax
from jax.sharding import PartitionSpec as P

HDIM = 128


def layer_norm(values, epsilon):
    center = values - jnp.mean(values, axis=-1, keepdims=True)
    spread = jnp.mean(center * center, axis=-1, keepdims=True)
    return center * lax.rsqrt(spread + epsilon)


def silu_round(values):
    return jax.nn.silu(values).astype(jnp.bfloat16)


def body(inputs, lengths, proj_in, proj_out):
    context_size = lax.axis_size("ctx")
    own_index = lax.axis_index("ctx")
    block_total, stripe, width_part = inputs.shape
    block_len = stripe * context_size
    row_count = 2 * block_len
    heads_dev = proj_in.shape[2] // HDIM
    reordered = jnp.stack([inputs[:context_size], inputs[context_size:][::-1]], axis=1)
    reordered = reordered.reshape(block_total, stripe, width_part)
    own_rows = lax.all_to_all(reordered, "ctx", split_axis=0, concat_axis=1, tiled=True)
    full_rows = lax.all_gather(own_rows, "head", axis=2, tiled=True)
    normed = layer_norm(full_rows.reshape(row_count, -1).astype(jnp.float32), 1e-06).astype(
        jnp.bfloat16
    )
    user_ends = jnp.cumsum(lengths)

    def segment(position):
        return jnp.sum((position[:, None] >= user_ends[None, :]).astype(jnp.int32), axis=1)

    offsets = jnp.arange(block_len, dtype=jnp.int32)
    own_blocks = jnp.stack([own_index, 2 * context_size - 1 - own_index])
    query_pos = (own_blocks[:, None] * block_len + offsets[None, :]).reshape(-1)
    query_seg = segment(query_pos)
    score_scale = 1.0 / math.sqrt(HDIM)
    projected = silu_round(
        jnp.einsum("rd,dgc->rgc", normed, proj_in, preferred_element_type=jnp.float32)
    )
    gating = projected[:, 0]
    queries = projected[:, 2]
    key_pair = (
        projected[:, 3].reshape(2, block_len, -1),
        projected[:, 1].reshape(2, block_len, -1),
    )

    def loader(shards, lead_row, tile_rows):
        key_rows = lax.dynamic_slice_in_dim(shards[0], lead_row, tile_rows, 0)
        value_rows = lax.dynamic_slice_in_dim(shards[1], lead_row, tile_rows, 0)
        return (
            key_rows.reshape(tile_rows * block_len, heads_dev, HDIM),
            value_rows.reshape(tile_rows * block_len, heads_dev, HDIM),
        )

    query_heads = queries.reshape(row_count, heads_dev, HDIM)
    zero_acc = jnp.zeros((row_count, heads_dev, HDIM), jnp.float32)
    shards = (
        lax.all_gather(key_pair[0], "ctx", axis=0, tiled=True),
        lax.all_gather(key_pair[1], "ctx", axis=0, tiled=True),
    )
    piece_rows = shards[0].shape[0]
    tile_rows = 4

    def one_tile(tile_index, partial_value):
        lead_row = tile_index * tile_rows
        listed = lead_row + jnp.arange(tile_rows, dtype=jnp.int32)
        holder = listed // 2
        block_ids = jnp.where(listed % 2 == 0, holder, 2 * context_size - 1 - holder)
        key_pos = (block_ids[:, None] * block_len + offsets[None, :]).reshape(-1)
        allowed = (query_seg[:, None] == segment(key_pos)[None, :]) & (
            key_pos[None, :] <= query_pos[:, None]
        )
        key_rows, value_rows = loader(shards, lead_row, tile_rows)
        scores = (
            jnp.einsum("qhd,khd->hqk", query_heads, key_rows, preferred_element_type=jnp.float32)
            * score_scale
        )
        weights = jnp.where(allowed[None], jax.nn.silu(scores), 0.0).astype(jnp.bfloat16)
        return partial_value + jnp.einsum(
            "hqk,khd->qhd", weights, value_rows, preferred_element_type=jnp.float32
        )

    attended = lax.fori_loop(0, piece_rows // tile_rows, one_tile, zero_acc)
    gate_prod = layer_norm(attended, 1e-05) * gating.reshape(row_count, heads_dev, HDIM).astype(
        jnp.float32
    )
    gate_prod = gate_prod.astype(jnp.bfloat16).reshape(row_count, -1)
    columns = lax.all_to_all(proj_out, "head", split_axis=1, concat_axis=0, tiled=True)
    summed = jnp.dot(
        lax.all_gather(gate_prod, "head", axis=1, tiled=True),
        columns,
        preferred_element_type=jnp.float32,
    )
    result = (own_rows.reshape(row_count, -1).astype(jnp.float32) + summed).astype(jnp.bfloat16)
    return result.reshape(1, 2, block_len, -1)


def solution(mesh):
    return jax.shard_map(
        body,
        mesh=mesh,
        in_specs=(P("dp", "ctx", "head"), P("dp"), P(None, None, "head"), P("head", None)),
        out_specs=P(("dp", "ctx"), None, None, "head"),
        check_vma=False,
    )
```

profile of v0, /device:TPU:0, one launch (start us, length us, event | category | flops | bytes accessed | tf_op | source)
XLA Modules:
  0.0 122.5 jit_solution(3696694843933152079)
XLA Ops:
  6.5 0.0 copy-start
  6.5 0.0 copy-start.2
  6.5 0.0 all-gather.3.cloned.1.call-start
  6.5 1.1 slice_bitcast_fusion
  7.7 9.2 %all_to_all.37 = bf16[4,128,256]{2,1,0:T(8,128)(2,1)S(1)} all-to-all(bf16[4,128,256]{2,1,0:T(8,128)(2,1)S(1)} %bitcast.59), channel_id=1, replica_groups=mesh['dp'=4,'ctx'=2,'head'=4] {'ctx'}, dimensions={0} | all-to-all | bytes 524288 | tf_op jit(solution)/shard_map/all_to_all | solution.py:29
  17.0 0.7 copy.34
  17.7 0.0 all-gather.3.cloned.1.call-update
  17.7 0.0 all-gather.5.cloned.1.call-start
  17.8 0.1 add_multiply_fusion
  17.9 0.1 add_bitcast_fusion.1
  17.9 0.1 add_bitcast_fusion
  18.0 0.0 copy-done.2
  18.0 0.2 reduce-window.8
  18.2 0.1 convert_reduce_fusion.2
  18.3 0.1 convert_reduce_fusion.1
  18.4 1.3 %compare_and_fusion = pred[512,1024]{1,0:T(8,128)(4,1)} fusion(s32[1024]{0:T(1024)S(1)} %bitcast.63, s32[1024]{0:T(1024)S(1)} %convert_reduce_fusion.1, s32[512]{0:T(512)S(1)} %bitcast.65, s32[512]{0:T(512)S(1)} %convert_reduce_fusion.2), kind=kLoop, calls=%fused_computation.8 | loop fusion | flops 1572864 | bytes 536576 | tf_op jit(solution)/shard_map/while/body/eval_jaxpr/and | solution.py:77
  19.7 28.5 %all-gather.3.cloned.1.call-done = bf16[2,256,1024]{2,1,0:T(8,128)(2,1)} async-done(((bf16[2,256,256]{2,1,0:T(8,128)(2,1)}), bf16[2,256,1024]{2,1,0:T(8,128)(2,1)}) %all-gather.3.cloned.1.call-update) | async-done | bytes 1048592 | tf_op jit(solution)/shard_map/all_gather | solution.py:30
  48.2 0.0 copy-start.1
  48.2 1.5 %convert_reduce_fusion = f32[2,256]{1,0:T(2,128)S(1)} fusion(bf16[2,256,1024]{2,1,0:T(8,128)(2,1)} %all-gather.3.cloned.1.call-done), kind=kLoop, calls=%fused_computation.14 | loop fusion | flops 1048064 | bytes 1050624 | tf_op jit(solution)/shard_map/reduce_sum | solution.py:11
  49.7 1.6 %multiply_reduce_fusion = f32[2,256]{1,0:T(2,128)S(1)} fusion(bf16[2,256,1024]{2,1,0:T(8,128)(2,1)} %all-gather.3.cloned.1.call-done, f32[2,256]{1,0:T(2,128)S(1)} %get-tuple-element.40), kind=kLoop, calls=%fused_computation.7 | loop fusion | flops 2096640 | bytes 1052672 | tf_op jit(solution)/shard_map/reduce_sum | solution.py:12
  51.4 0.0 copy-done.1
  51.4 0.3 fusion.1
  51.7 0.0 copy-done
  51.7 1.5 %multiply_convert_fusion = bf16[512,4,256]{2,0,1:T(8,128)(2,1)S(1)} fusion(bf16[1024,4,256]{2,1,0:T(4,128)(2,1)S(1)} %copy-done, bf16[512,1024]{1,0:T(8,128)(2,1)S(1)} %fusion.1), kind=kOutput, calls=%fused_computation.6 | convolution fusion | flops 1076363264 | bytes 4194304 | tf_op jit(solution)/shard_map/rd,dgc->rgc/dot_general | solution.py:45
  53.2 0.9 fusion.22
  54.1 7.7 %all_gather.14 = bf16[4,256,256]{2,1,0:T(8,128)(2,1)S(1)} all-gather(bf16[2,256,256]{2,1,0:T(8,128)(2,1)S(1)} %bitcast.56), channel_id=1, replica_groups=mesh['dp'=4,'ctx'=2,'head'=4] {'ctx'}, dimensions={0}, use_global_device_ids=true | all-gather | bytes 786432 | tf_op jit(solution)/shard_map/all_gather | solution.py:65
  61.8 0.9 reshape.244
  62.7 7.9 %all_gather.13 = bf16[4,256,256]{2,1,0:T(8,128)(2,1)S(1)} all-gather(bf16[2,256,256]{2,1,0:T(8,128)(2,1)S(1)} %bitcast.55), channel_id=1, replica_groups=mesh['dp'=4,'ctx'=2,'head'=4] {'ctx'}, dimensions={0}, use_global_device_ids=true | all-gather | bytes 786432 | tf_op jit(solution)/shard_map/all_gather | solution.py:66
  70.6 0.9 reshape.251
  71.5 0.1 reshape_squeeze.11
  71.6 3.5 %fusion.23 = (f32[512,2]{0,1:T(2,128)S(1)}, f32[512,2,128]{0,2,1:T(8,128)S(1)}) fusion(pred[512,1024]{1,0:T(8,128)(4,1)} %compare_and_fusion, bf16[1024,2,128]{2,1,0:T(2,128)(2,1)} %reshape.244, bf16[512,2,128]{2,1,0:T(2,128)(2,1)S(1)} %reshape_squeeze.11, bf16[1024,2,128]{2,1,0:T(2,128)(2,1)} %reshape.251), kind=kOutput, calls=%fused_computation.45 | convolution fusion | flops 544340992 | bytes 2363392 | tf_op jit(solution)/shard_map/while/body/eval_jaxpr/hqk,khd->qhd/dot_general | solution.py:86
  75.1 0.1 multiply_reduce_fusion.1
  75.2 1.2 %copy.43 = f32[512,1,256]{0,2,1:T(8,128)S(1)} copy(f32[512,1,256]{2,0,1:T(8,128)} %get-tuple-element.24) | data formatting | bytes 1048576 | tf_op jit(solution)/shard_map/convert_element_type | solution.py:91
  76.5 0.8 multiply_convert_fusion.1
  77.3 0.0 all-gather.5.cloned.1.call-update
  77.3 2.1 %copy.40 = bf16[256,1024]{0,1:T(8,128)(2,1)} copy(bf16[256,1024]{1,0:T(8,128)(2,1)} %param.7) | data formatting | bytes 1048576 | tf_op args[3]
  79.4 3.5 %all-to-all-start.1 = ((bf16[256,4,256]{0,2,1:T(8,128)(2,1)}), bf16[256,4,256]{0,2,1:T(8,128)(2,1)S(1)}, u32[]{:S(2)}, u32[]{:S(2)}) async-start(bf16[256,4,256]{0,2,1:T(8,128)(2,1)} %bitcast.19), calls=%async_computation.1 | async-start | bytes 1048576 | tf_op jit(solution)/shard_map/all_to_all | solution.py:95
  82.9 25.4 %all-to-all-done.1 = bf16[256,4,256]{0,2,1:T(8,128)(2,1)S(1)} async-done(((bf16[256,4,256]{0,2,1:T(8,128)(2,1)}), bf16[256,4,256]{0,2,1:T(8,128)(2,1)S(1)}, u32[]{:S(2)}, u32[]{:S(2)}) %all-to-all-start.1) | async-done | bytes 524320 | tf_op jit(solution)/shard_map/all_to_all | solution.py:95
  108.4 1.0 copy.41
  109.4 3.7 %all-gather.5.cloned.1.call-done = bf16[512,1024]{0,1:T(8,128)(2,1)} async-done(((bf16[512,256]{0,1:T(8,128)(2,1)}), bf16[512,1024]{0,1:T(8,128)(2,1)}) %all-gather.5.cloned.1.call-update) | async-done | bytes 1048592 | tf_op jit(solution)/shard_map/all_gather | solution.py:97
  113.1 2.5 %fusion.6 = bf16[512,256]{1,0:T(8,128)(2,1)} fusion(f32[512,256]{1,0:T(8,128)S(1)} %bitcast.60, bf16[512,1024]{0,1:T(8,128)(2,1)} %all-gather.5.cloned.1.call-done, bf16[1024,256]{1,0:T(8,128)(2,1)} %bitcast.61), kind=kOutput, calls=%fused_computation.12 | convolution fusion | flops 268697600 | bytes 2359296 | tf_op jit(solution)/shard_map/dot_general | solution.py:96
  (12 shorter events, 0.1 us)
Async XLA Ops:
  6.5 45.2 %copy-start = (bf16[1024,4,256]{2,1,0:T(4,128)(2,1)S(1)}, bf16[1024,4,256]{2,1,0:T(4,128)(2,1)}, u32[]{:S(2)}) copy-start(bf16[1024,4,256]{2,1,0:T(4,128)(2,1)} %param.6) | copy-start | bytes 6291460
  6.5 11.5 %copy-start.2 = (s32[4]{0:T(128)S(1)}, s32[4]{0:T(128)}, u32[]{:S(2)}) copy-start(s32[4]{0:T(128)} %param.5) | copy-start | bytes 52
  6.5 41.6 %all-gather.3.cloned.1.call-start = ((), (), s32[]{:S(2)}) async-start(), calls=%async_computation.2 | async-start | bytes 1310720 | tf_op jit(solution)/shard_map/all_gather | solution.py:30
  17.7 95.4 %all-gather.5.cloned.1.call-start = ((), (), s32[]{:S(2)}) async-start(), calls=%async_computation.3 | async-start | bytes 1310720 | tf_op jit(solution)/shard_map/all_gather | solution.py:97
  48.2 3.2 %copy-start.1 = (bf16[2,256,1024]{2,1,0:T(8,128)(2,1)S(1)}, bf16[2,256,1024]{2,1,0:T(8,128)(2,1)}, u32[]{:S(2)}) copy-start(bf16[2,256,1024]{2,1,0:T(8,128)(2,1)} %all-gather.3.cloned.1.call-done) | copy-start | bytes 3145732
  79.4 29.0 %all-to-all-start.1 = ((bf16[256,4,256]{0,2,1:T(8,128)(2,1)}), bf16[256,4,256]{0,2,1:T(8,128)(2,1)S(1)}, u32[]{:S(2)}, u32[]{:S(2)}) async-start(bf16[256,4,256]{0,2,1:T(8,128)(2,1)} %bitcast.19), calls=%async_computation.1 | async-start | bytes 1048576 | tf_op jit(solution)/shard_map/all_to_all | solution.py:95
Sparse Core Ops, SparseCore 0:
  17.8 30.2 all-gather.2
  77.4 35.6 all-gather.4
where the time goes:
time: 123 us; the launch traced here: 122 us
  waiting for transfers between devices  57.7 us (47%)
  blocking collectives  24.8 us (20%)
  between operations  13.5 us (11%)
  local copies, waits for them, and re-layouts  8.2 us (7%)
  matrix products  7.57 us (6%)
  other arithmetic  7.19 us (6%)
  starting transfers between devices  3.51 us (3%)
    all_gather x1, waiting for transfers between devices, body(): full_rows = lax.all_gather(own_rows, 'head', axis=2, tiled=True)  28.5 us
    all_to_all x1, waiting for transfers between devices, body(): lax.all_to_all(proj_out, 'head', split_axis=1, concat_axis=0, tiled=True)  25.4 us
    all_to_all x1, blocking collectives, body(): lax.all_to_all(reordered, 'ctx', split_axis=0, concat_axis=1, tiled=True)  9.24 us
    all_gather x1, blocking collectives, body(): lax.all_gather(key_pair[1], 'ctx', axis=0, tiled=True)  7.86 us
    all_gather x1, blocking collectives, body(): lax.all_gather(key_pair[0], 'ctx', axis=0, tiled=True)  7.68 us
    all_gather x1, waiting for transfers between devices, body(): lax.all_gather(gate_prod, 'head', axis=1, tiled=True)  3.71 us
    dot_general x1, matrix products, one_tile(): jnp.einsum('hqk,khd->qhd', weights, value_rows, preferred_element_type=jn...  3.53 us
    all_to_all x1, starting transfers between devices, body(): lax.all_to_all(proj_out, 'head', split_axis=1, concat_axis=0, tiled=True)  3.47 us
  transfers between devices with their start and end apart: 3, of which 3 were waited for; matrix products, arithmetic and copies ran while one was open for 4% of the time, Pallas kernels for 0%

commit v1 on v0

--- a/solution.py
+++ b/solution.py
@@ -27,7 +27,24 @@
     reordered = jnp.stack([inputs[:context_size], inputs[context_size:][::-1]], axis=1)
     reordered = reordered.reshape(block_total, stripe, width_part)
     own_rows = lax.all_to_all(reordered, "ctx", split_axis=0, concat_axis=1, tiled=True)
-    full_rows = lax.all_gather(own_rows, "head", axis=2, tiled=True)
+    ways, here, step = (lax.axis_size("head"), lax.axis_index("head"), own_rows.shape[2])
+    shape = [n * ways if d == 2 else n for d, n in enumerate(own_rows.shape)]
+    full_rows = lax.dynamic_update_slice_in_dim(
+        jnp.zeros(shape, own_rows.dtype), own_rows, here * step, axis=2
+    )
+    going_up = going_down = own_rows
+    for far in range(1, ways // 2 + 1):
+        going_up = lax.ppermute(going_up, "head", [(d, (d + 1) % ways) for d in range(ways)])
+        full_rows = lax.dynamic_update_slice_in_dim(
+            full_rows, going_up, (here - far) % ways * step, axis=2
+        )
+        if 2 * far < ways:
+            going_down = lax.ppermute(
+                going_down, "head", [(d, (d - 1) % ways) for d in range(ways)]
+            )
+            full_rows = lax.dynamic_update_slice_in_dim(
+                full_rows, going_down, (here + far) % ways * step, axis=2
+            )
     normed = layer_norm(full_rows.reshape(row_count, -1).astype(jnp.float32), 1e-06).astype(
         jnp.bfloat16
     )

time: 123 us -> 107 us (0.87)
  waiting for transfers between devices: 57.7 us -> 44.7 us
  blocking collectives: 24.8 us -> 14.1 us
  starting transfers between devices: 3.51 us -> 13.2 us
    all_gather x1 -> x0, waiting for transfers between devices: 28.5 us -> none  [body(): full_rows = lax.all_gather(own_rows, 'head', axis=2, tiled=True)]
    ppermute x0 -> x3, waiting for transfers between devices: none -> 13.6 us  [the longest x2 10.7 us: body(): lax.ppermute(going_up, 'head', [(d, (d + 1) % ways) for d in range(ways)])]
    all_to_all x1 -> x0, blocking collectives: 9.24 us -> none  [body(): lax.all_to_all(reordered, 'ctx', split_axis=0, concat_axis=1, tiled=True)]
    ppermute x0 -> x3, starting transfers between devices: none -> 5.42 us  [the longest x2 3.38 us: body(): lax.ppermute(going_up, 'head', [(d, (d + 1) % ways) for d in range(ways)])]
    all_to_all x0 -> x1, waiting for transfers between devices: none -> 4.72 us  [body(): lax.all_to_all(reordered, 'ctx', split_axis=0, concat_axis=1, tiled=True)]
    all_to_all x0 -> x1, starting transfers between devices: none -> 4.26 us  [body(): lax.all_to_all(reordered, 'ctx', split_axis=0, concat_axis=1, tiled=True)]
    all_to_all x1, waiting for transfers between devices: 25.4 us -> 22 us  [body(): lax.all_to_all(proj_out, 'head', split_axis=1, concat_axis=0, tiled=True)]
    reduce_sum x1, other arithmetic: 1.52 us -> 0.21 us  [layer_norm(): center = values - jnp.mean(values, axis=-1, keepdims=True)]
  transfers between devices with their start and end apart: 3 -> 6, of which waited for: 3 -> 6; matrix products, arithmetic and copies ran while one was open for 4% -> 5% of each run, Pallas kernels for 0% -> 0%
where the time goes in v1:
time: 107 us
  waiting for transfers between devices  44.7 us (42%)
  blocking collectives  14.1 us (13%)
  between operations  13.5 us (13%)
  starting transfers between devices  13.2 us (12%)
  local copies, waits for them, and re-layouts  7.71 us (7%)
  matrix products  7.58 us (7%)
  other arithmetic  6 us (6%)
    all_to_all x1, waiting for transfers between devices, body(): lax.all_to_all(proj_out, 'head', split_axis=1, concat_axis=0, tiled=True)  22 us
    ppermute x2, waiting for transfers between devices, body(): lax.ppermute(going_up, 'head', [(d, (d + 1) % ways) for d in range(ways)])  10.7 us
    all_gather x1, blocking collectives, body(): lax.all_gather(key_pair[0], 'ctx', axis=0, tiled=True)  7.03 us
    all_gather x1, blocking collectives, body(): lax.all_gather(key_pair[1], 'ctx', axis=0, tiled=True)  7.03 us
    all_to_all x1, waiting for transfers between devices, body(): lax.all_to_all(reordered, 'ctx', split_axis=0, concat_axis=1, tiled=True)  4.72 us
    all_gather x1, waiting for transfers between devices, body(): lax.all_gather(gate_prod, 'head', axis=1, tiled=True)  4.34 us
    all_to_all x1, starting transfers between devices, body(): lax.all_to_all(reordered, 'ctx', split_axis=0, concat_axis=1, tiled=True)  4.26 us
    dot_general x1, matrix products, one_tile(): jnp.einsum('hqk,khd->qhd', weights, value_rows, preferred_element_type=jn...  3.54 us
  transfers between devices with their start and end apart: 6, of which 6 were waited for; matrix products, arithmetic and copies ran while one was open for 5% of the time, Pallas kernels for 0%

profile of v1, /device:TPU:0, one launch (start us, length us, event | category | flops | bytes accessed | tf_op | source)
XLA Modules:
  0.0 106.7 jit_solution(16951041970413681814)
XLA Ops:
  6.5 0.0 copy-start
  6.5 1.1 %slice_bitcast_fusion = (bf16[2,1,128,256]{3,2,1,0:T(8,128)(2,1)S(1)}, bf16[2,128,256]{2,1,0:T(8,128)(2,1)S(1)}) fusion(bf16[4,128,256]{2,1,0:T(8,128)(2,1)} %param.4), kind=kLoop, calls=%fused_computation.23 | loop fusion | bytes 524288 | tf_op jit(solution)/shard_map/stack | solution.py:27
  7.7 0.7 pad_maximum_fusion
  8.4 4.3 %all-to-all-start = ((bf16[4,128,256]{2,1,0:T(8,128)(2,1)}), bf16[4,128,256]{2,1,0:T(8,128)(2,1)S(1)}, u32[]{:S(2)}, u32[]{:S(2)}) async-start(bf16[4,128,256]{2,1,0:T(8,128)(2,1)} %bitcast.2), calls=%async_computation | async-start | bytes 524288 | tf_op jit(solution)/shard_map/all_to_all | solution.py:29
  12.7 0.0 all-gather.2.cloned.1.call-start
  12.7 0.1 add_bitcast_fusion
  12.8 0.1 add_multiply_fusion
  12.8 0.1 add_bitcast_fusion.1
  12.9 0.8 reduce-window.8
  13.8 0.1 convert_reduce_fusion.1
  13.8 4.7 %all-to-all-done = bf16[4,128,256]{2,1,0:T(8,128)(2,1)S(1)} async-done(((bf16[4,128,256]{2,1,0:T(8,128)(2,1)}), bf16[4,128,256]{2,1,0:T(8,128)(2,1)S(1)}, u32[]{:S(2)}, u32[]{:S(2)}) %all-to-all-start) | async-done | bytes 262176 | tf_op jit(solution)/shard_map/all_to_all | solution.py:29
  18.6 1.8 %collective-permute-start = (bf16[2,256,256]{2,1,0:T(8,128)(2,1)S(1)}, bf16[2,256,256]{2,1,0:T(8,128)(2,1)S(1)}, u32[]{:S(2)}, u32[]{:S(2)}) collective-permute-start(bf16[2,256,256]{2,1,0:T(8,128)(2,1)S(1)} %bitcast.58), channel_id=1, source_target_pairs={{0,1},{1,2},{2,3},{3,0},{4,5},{5,6},{6,7},{7,4},{8,9},{9,10},{10,1... | collective-permute-start | bytes 786440 | tf_op jit(solution)/shard_map/ppermute | solution.py:37
  20.4 0.1 convert_reduce_fusion.2
  20.5 2.0 %collective-permute-start.1 = (bf16[2,256,256]{2,1,0:T(8,128)(2,1)S(1)}, bf16[2,256,256]{2,1,0:T(8,128)(2,1)S(1)}, u32[]{:S(2)}, u32[]{:S(2)}) collective-permute-start(bf16[2,256,256]{2,1,0:T(8,128)(2,1)S(1)} %bitcast.59), channel_id=1, source_target_pairs={{0,3},{1,0},{2,1},{3,2},{4,7},{5,4},{6,5},{7,6},{8,11},{9,8},{10,9... | collective-permute-start | bytes 786440 | tf_op jit(solution)/shard_map/ppermute | solution.py:42
  22.6 1.3 %compare_and_fusion = pred[512,1024]{1,0:T(8,128)(4,1)} fusion(s32[1024]{0:T(1024)S(1)} %bitcast.64, s32[1024]{0:T(1024)S(1)} %convert_reduce_fusion.1, s32[512]{0:T(512)S(1)} %bitcast.66, s32[512]{0:T(512)S(1)} %convert_reduce_fusion.2), kind=kLoop, calls=%fused_computation.8 | loop fusion | flops 1572864 | bytes 536576 | tf_op jit(solution)/shard_map/while/body/eval_jaxpr/and | solution.py:94
  23.9 5.8 %collective-permute-done = bf16[2,256,256]{2,1,0:T(8,128)(2,1)S(1)} collective-permute-done((bf16[2,256,256]{2,1,0:T(8,128)(2,1)S(1)}, bf16[2,256,256]{2,1,0:T(8,128)(2,1)S(1)}, u32[]{:S(2)}, u32[]{:S(2)}) %collective-permute-start) | collective-permute-done | bytes 262176 | tf_op jit(solution)/shard_map/ppermute | solution.py:37
  29.7 1.5 %collective-permute-start.2 = (bf16[2,256,256]{2,1,0:T(8,128)(2,1)S(1)}, bf16[2,256,256]{2,1,0:T(8,128)(2,1)S(1)}, u32[]{:S(2)}, u32[]{:S(2)}) collective-permute-start(bf16[2,256,256]{2,1,0:T(8,128)(2,1)S(1)} %collective-permute-done), channel_id=1, source_target_pairs={{0,1},{1,2},{2,3},{3,0},{4,5},{5,6},{6,7},{7,4},{8,9},{9,10},{10,1... | collective-permute-start | bytes 786440 | tf_op jit(solution)/shard_map/ppermute | solution.py:37
  31.2 0.1 broadcast_in_dim.39
  31.4 2.8 %collective-permute-done.1 = bf16[2,256,256]{2,1,0:T(8,128)(2,1)S(1)} collective-permute-done((bf16[2,256,256]{2,1,0:T(8,128)(2,1)S(1)}, bf16[2,256,256]{2,1,0:T(8,128)(2,1)S(1)}, u32[]{:S(2)}, u32[]{:S(2)}) %collective-permute-start.1) | collective-permute-done | bytes 262176 | tf_op jit(solution)/shard_map/ppermute | solution.py:42
  34.3 4.9 %collective-permute-done.2 = bf16[2,256,256]{2,1,0:T(8,128)(2,1)S(1)} collective-permute-done((bf16[2,256,256]{2,1,0:T(8,128)(2,1)S(1)}, bf16[2,256,256]{2,1,0:T(8,128)(2,1)S(1)}, u32[]{:S(2)}, u32[]{:S(2)}) %collective-permute-start.2) | collective-permute-done | bytes 262176 | tf_op jit(solution)/shard_map/ppermute | solution.py:37
  39.2 0.2 convert_reduce_fusion
  39.4 0.4 multiply_reduce_fusion
  39.9 0.3 fusion.1
  40.2 0.0 copy-done
  40.2 1.5 %multiply_convert_fusion = bf16[512,4,256]{2,0,1:T(8,128)(2,1)S(1)} fusion(bf16[1024,4,256]{2,1,0:T(4,128)(2,1)S(1)} %copy-done, bf16[512,1024]{1,0:T(8,128)(2,1)S(1)} %fusion.1), kind=kOutput, calls=%fused_computation.6 | convolution fusion | flops 1076363264 | bytes 4194304 | tf_op jit(solution)/shard_map/rd,dgc->rgc/dot_general | solution.py:62
  41.7 0.9 fusion.22
  42.6 7.0 %all_gather.10 = bf16[4,256,256]{2,1,0:T(8,128)(2,1)S(1)} all-gather(bf16[2,256,256]{2,1,0:T(8,128)(2,1)S(1)} %bitcast.56), channel_id=1, replica_groups=mesh['dp'=4,'ctx'=2,'head'=4] {'ctx'}, dimensions={0}, use_global_device_ids=true | all-gather | bytes 786432 | tf_op jit(solution)/shard_map/all_gather | solution.py:82
  49.6 0.9 reshape.244
  50.6 7.0 %all_gather.9 = bf16[4,256,256]{2,1,0:T(8,128)(2,1)S(1)} all-gather(bf16[2,256,256]{2,1,0:T(8,128)(2,1)S(1)} %bitcast.55), channel_id=1, replica_groups=mesh['dp'=4,'ctx'=2,'head'=4] {'ctx'}, dimensions={0}, use_global_device_ids=true | all-gather | bytes 786432 | tf_op jit(solution)/shard_map/all_gather | solution.py:83
  57.6 0.9 reshape.251
  58.5 0.1 reshape_squeeze.11
  58.6 3.5 %fusion.23 = (f32[512,2]{0,1:T(2,128)S(1)}, f32[512,2,128]{0,2,1:T(8,128)S(1)}) fusion(pred[512,1024]{1,0:T(8,128)(4,1)} %compare_and_fusion, bf16[1024,2,128]{2,1,0:T(2,128)(2,1)} %reshape.244, bf16[512,2,128]{2,1,0:T(2,128)(2,1)S(1)} %reshape_squeeze.11, bf16[1024,2,128]{2,1,0:T(2,128)(2,1)} %reshape.251), kind=kOutput, calls=%fused_computation.49 | convolution fusion | flops 544340992 | bytes 2363392 | tf_op jit(solution)/shard_map/while/body/eval_jaxpr/hqk,khd->qhd/dot_general | solution.py:103
  62.2 0.1 multiply_reduce_fusion.1
  62.3 1.2 %copy.43 = f32[512,1,256]{0,2,1:T(8,128)S(1)} copy(f32[512,1,256]{2,0,1:T(8,128)} %get-tuple-element.24) | data formatting | bytes 1048576 | tf_op jit(solution)/shard_map/convert_element_type | solution.py:108
  63.5 0.8 multiply_convert_fusion.1
  64.3 0.0 all-gather.2.cloned.1.call-update
  64.3 2.1 %copy.40 = bf16[256,1024]{0,1:T(8,128)(2,1)} copy(bf16[256,1024]{1,0:T(8,128)(2,1)} %param.7) | data formatting | bytes 1048576 | tf_op args[3]
  66.4 3.5 %all-to-all-start.1 = ((bf16[256,4,256]{0,2,1:T(8,128)(2,1)}), bf16[256,4,256]{0,2,1:T(8,128)(2,1)S(1)}, u32[]{:S(2)}, u32[]{:S(2)}) async-start(bf16[256,4,256]{0,2,1:T(8,128)(2,1)} %bitcast.19), calls=%async_computation.1 | async-start | bytes 1048576 | tf_op jit(solution)/shard_map/all_to_all | solution.py:112
  69.9 22.0 %all-to-all-done.1 = bf16[256,4,256]{0,2,1:T(8,128)(2,1)S(1)} async-done(((bf16[256,4,256]{0,2,1:T(8,128)(2,1)}), bf16[256,4,256]{0,2,1:T(8,128)(2,1)S(1)}, u32[]{:S(2)}, u32[]{:S(2)}) %all-to-all-start.1) | async-done | bytes 524320 | tf_op jit(solution)/shard_map/all_to_all | solution.py:112
  91.9 1.0 copy.41
  93.0 4.3 %all-gather.2.cloned.1.call-done = bf16[512,1024]{0,1:T(8,128)(2,1)} async-done(((bf16[512,256]{0,1:T(8,128)(2,1)}), bf16[512,1024]{0,1:T(8,128)(2,1)}) %all-gather.2.cloned.1.call-update) | async-done | bytes 1048592 | tf_op jit(solution)/shard_map/all_gather | solution.py:114
  97.3 2.5 %fusion.6 = bf16[512,256]{1,0:T(8,128)(2,1)} fusion(f32[512,256]{1,0:T(8,128)S(1)} %bitcast.61, bf16[512,1024]{0,1:T(8,128)(2,1)} %all-gather.2.cloned.1.call-done, bf16[1024,256]{1,0:T(8,128)(2,1)} %bitcast.62), kind=kOutput, calls=%fused_computation.12 | convolution fusion | flops 268697600 | bytes 2359296 | tf_op jit(solution)/shard_map/dot_general | solution.py:113
  (16 shorter events, 0.2 us)
Async XLA Ops:
  6.5 33.7 %copy-start = (bf16[1024,4,256]{2,1,0:T(4,128)(2,1)S(1)}, bf16[1024,4,256]{2,1,0:T(4,128)(2,1)}, u32[]{:S(2)}) copy-start(bf16[1024,4,256]{2,1,0:T(4,128)(2,1)} %param.6) | copy-start | bytes 6291460
  8.4 10.1 %all-to-all-start = ((bf16[4,128,256]{2,1,0:T(8,128)(2,1)}), bf16[4,128,256]{2,1,0:T(8,128)(2,1)S(1)}, u32[]{:S(2)}, u32[]{:S(2)}) async-start(bf16[4,128,256]{2,1,0:T(8,128)(2,1)} %bitcast.2), calls=%async_computation | async-start | bytes 524288 | tf_op jit(solution)/shard_map/all_to_all | solution.py:29
  12.7 84.6 %all-gather.2.cloned.1.call-start = ((), (), s32[]{:S(2)}) async-start(), calls=%async_computation.2 | async-start | bytes 1310720 | tf_op jit(solution)/shard_map/all_gather | solution.py:114
  18.6 11.1 %collective-permute-start = (bf16[2,256,256]{2,1,0:T(8,128)(2,1)S(1)}, bf16[2,256,256]{2,1,0:T(8,128)(2,1)S(1)}, u32[]{:S(2)}, u32[]{:S(2)}) collective-permute-start(bf16[2,256,256]{2,1,0:T(8,128)(2,1)S(1)} %bitcast.58), channel_id=1, source_target_pairs={{0,1},{1,2},{2,3},{3,0},{4,5},{5,6},{6,7},{7,4},{8,9},{9,10},{10,1... | collective-permute-start | bytes 786440 | tf_op jit(solution)/shard_map/ppermute | solution.py:37
  20.5 13.7 %collective-permute-start.1 = (bf16[2,256,256]{2,1,0:T(8,128)(2,1)S(1)}, bf16[2,256,256]{2,1,0:T(8,128)(2,1)S(1)}, u32[]{:S(2)}, u32[]{:S(2)}) collective-permute-start(bf16[2,256,256]{2,1,0:T(8,128)(2,1)S(1)} %bitcast.59), channel_id=1, source_target_pairs={{0,3},{1,0},{2,1},{3,2},{4,7},{5,4},{6,5},{7,6},{8,11},{9,8},{10,9... | collective-permute-start | bytes 786440 | tf_op jit(solution)/shard_map/ppermute | solution.py:42
  29.7 9.5 %collective-permute-start.2 = (bf16[2,256,256]{2,1,0:T(8,128)(2,1)S(1)}, bf16[2,256,256]{2,1,0:T(8,128)(2,1)S(1)}, u32[]{:S(2)}, u32[]{:S(2)}) collective-permute-start(bf16[2,256,256]{2,1,0:T(8,128)(2,1)S(1)} %collective-permute-done), channel_id=1, source_target_pairs={{0,1},{1,2},{2,3},{3,0},{4,5},{5,6},{6,7},{7,4},{8,9},{9,10},{10,1... | collective-permute-start | bytes 786440 | tf_op jit(solution)/shard_map/ppermute | solution.py:37
  66.4 25.5 %all-to-all-start.1 = ((bf16[256,4,256]{0,2,1:T(8,128)(2,1)}), bf16[256,4,256]{0,2,1:T(8,128)(2,1)S(1)}, u32[]{:S(2)}, u32[]{:S(2)}) async-start(bf16[256,4,256]{0,2,1:T(8,128)(2,1)} %bitcast.19), calls=%async_computation.1 | async-start | bytes 1048576 | tf_op jit(solution)/shard_map/all_to_all | solution.py:112
Sparse Core Ops, SparseCore 0:
  64.5 32.8 all-gather.1
